TPU v7x, 256 devices: a whole 4x4x8 slice. The times are simulated.
256 devices in a mesh: lat: 8 (over z_lo, core), lon: 8 (over z_hi, x), chan: 4 (over y).
Axes of the slice: x: 4, y: 4, z: 8 (z_hi: 2, z_lo: 4; z = z_hi * 4 + z_lo), core: 2. Of those that a mesh axis runs over, the one named last changes fastest.
Arguments:
- queries: bfloat16 [128, 64, 2560], P('lat', 'lon', 'chan'), may hold values from -8 to 8
- keys: bfloat16 [128, 64, 2560], P('lat', 'lon', 'chan'), may hold values from -8 to 8
- values: bfloat16 [128, 64, 2560], P('lat', 'lon', 'chan'), may hold values from -6 to 6
- attn_out: bfloat16 [128, 64, 2560], P('lat', 'lon', 'chan'), may hold values from -6 to 6
- grad_out: bfloat16 [128, 64, 5120], P('lat', 'lon', 'chan'), may hold values from -6 to 6
- w_out: bfloat16 [5120, 2560], P(('lat', 'lon'), 'chan'), may hold values from -0.078125 to 0.078125
- bias_table: float32 [20, 25, 13], P('chan'), may hold values from -5 to 5
- key_mask: int32 [128, 64], replicated, may hold values 0 or 1
Outputs:
- grad_queries: bfloat16 [128, 64, 2560], P('lat', 'lon', 'chan')
- grad_keys: bfloat16 [128, 64, 2560], P('lat', 'lon', 'chan')
- grad_values: bfloat16 [128, 64, 2560], P('lat', 'lon', 'chan')
- grad_wout: float32 [5120, 2560], P(('lat', 'lon'), 'chan')
- grad_table: float32 [20, 25, 13], P('chan')
All inputs are finite; a program needn't handle non-finite values.
Results may differ from a plain program's by a relative error of at most 0.007.
Values may be sent and summed in bfloat16 or wider, within the bound.
No kernel may reach another device: no remote copies, remote signals or barrier semaphores. Data moves between devices by JAX's collectives and lax.ppermute only.
A program may use at most 128 MiB of HBM per device.

v0:
```python
import jax
import jax.numpy as jnp
from jax import lax
from jax.sharding import PartitionSpec as P

HEAD_DIM = 128
WIN = 13


def extended_2(value, sides, width, wrap):
    for axis, dim in sides:
        count, length = (lax.axis_size(axis), value.shape[dim])
        up = [(i, (i + 1) % count) for i in range(count if wrap else count - 1)]
        down = [(j, i) for i, j in up]
        last = lax.slice_in_dim(value, length - width, length, axis=dim)
        leading = lax.slice_in_dim(value, 0, width, axis=dim)
        before = lax.ppermute(last, axis, up)
        after = lax.ppermute(leading, axis, down)
        value = jnp.concatenate([before, value, after], axis=dim)
    return value


def fold_lon(extended, core_width):
    full_width = extended.shape[2]
    reach_cells = (full_width - core_width) // 2
    rim_cells = jnp.concatenate(
        [extended[:, :, :reach_cells], extended[:, :, full_width - reach_cells :]], axis=2
    )
    received = extended_2(rim_cells.astype(jnp.bfloat16), (("lon", 2),), reach_cells, True).astype(
        rim_cells.dtype
    )
    middle = extended[:, :, reach_cells : full_width - reach_cells]
    front_add = jnp.pad(
        received[:, :, :reach_cells], ((0, 0), (0, 0), (0, core_width - reach_cells), (0, 0))
    )
    back_add = jnp.pad(
        received[:, :, 3 * reach_cells :], ((0, 0), (0, 0), (core_width - reach_cells, 0), (0, 0))
    )
    return middle + front_add + back_add


def fold_lat(extended, core_width):
    full_width = extended.shape[1]
    reach_cells = (full_width - core_width) // 2
    rim_cells = jnp.concatenate(
        [extended[:, :reach_cells], extended[:, full_width - reach_cells :]], axis=1
    )
    received = extended_2(rim_cells.astype(jnp.bfloat16), (("lat", 1),), reach_cells, False).astype(
        rim_cells.dtype
    )
    middle = extended[:, reach_cells : full_width - reach_cells]
    front_add = jnp.pad(
        received[:, :reach_cells], ((0, 0), (0, core_width - reach_cells), (0, 0), (0, 0))
    )
    back_add = jnp.pad(
        received[:, 3 * reach_cells :], ((0, 0), (core_width - reach_cells, 0), (0, 0), (0, 0))
    )
    return middle + front_add + back_add


def local(queries, keys, values, attn_out, grad_out, w_out, bias_table, key_mask):
    lat_rows, lon_cols, chan_width = queries.shape
    head_count = bias_table.shape[0]
    reach_cells = WIN // 2
    score_scale = HEAD_DIM ** (-0.5)
    tokens = lat_rows * lon_cols
    ext_rows = lat_rows + 2 * reach_cells
    ext_cols = lon_cols + 2 * reach_cells
    row_block = 4
    key_span = row_block + WIN - 1
    block_count = lat_rows // row_block
    block_rows = row_block * lon_cols
    block_keys = key_span * ext_cols
    offset_rows = 2 * WIN - 1
    low_pad = row_block - 1
    lat_total = lat_rows * lax.axis_size("lat")
    lon_total = lon_cols * lax.axis_size("lon")
    contract_lead = (((0,), (0,)), ((), ()))
    full_grad = lax.all_gather(grad_out, "chan", axis=2, tiled=True).reshape(tokens, -1)
    grad_cols = jnp.transpose(full_grad)
    slab_part = grad_cols
    grad_attn = lax.dot_general(
        slab_part,
        lax.all_gather(w_out, ("lat", "lon"), axis=0, tiled=True),
        contract_lead,
        preferred_element_type=jnp.float32,
    ).astype(jnp.bfloat16)
    kv_pair = jnp.stack([keys, values])
    extended = extended_2(kv_pair, (("lat", 1), ("lon", 2)), reach_cells, True)
    lat_first = lax.axis_index("lat") * lat_rows
    lon_first = lax.axis_index("lon") * lon_cols
    ext_col = lon_first - reach_cells + jnp.arange(ext_cols, dtype=jnp.int32)
    wrap_col = ext_col % lon_total
    mask_cols = jnp.take(key_mask, wrap_col, axis=1)
    mark_cols = wrap_col % 4 == 0
    rel_lon = (
        jnp.arange(ext_cols, dtype=jnp.int32)[None, :]
        - jnp.arange(lon_cols, dtype=jnp.int32)[:, None]
    )
    in_lon = (rel_lon >= 0) & (rel_lon < WIN)
    lon_pick = jnp.clip(rel_lon, 0, WIN - 1)
    lon_table = jnp.take(bias_table, lon_pick, axis=2).transpose(0, 2, 1, 3)
    table_pad = jnp.pad(lon_table, ((0, 0), (0, 0), (low_pad, low_pad), (0, 0)))
    query_heads = queries.reshape(lat_rows, lon_cols, head_count, HEAD_DIM)
    grad_heads = grad_attn.reshape(lat_rows, lon_cols, head_count, HEAD_DIM)

    def block_step(state_pair, block_index):
        grad_pair, table_acc = state_pair
        local_first = block_index * row_block
        top_row = lat_first + local_first
        key_first = jnp.clip(top_row - reach_cells, 0, lat_total - key_span)
        key_local = key_first - (lat_first - reach_cells)
        query_rows = top_row + jnp.arange(row_block, dtype=jnp.int32)
        window_first = jnp.clip(query_rows - reach_cells, 0, lat_total - WIN)
        key_glob = key_first + jnp.arange(key_span, dtype=jnp.int32)
        in_lat = (key_glob[None, :] >= window_first[:, None]) & (
            key_glob[None, :] < window_first[:, None] + WIN
        )
        mask_rows = lax.dynamic_slice_in_dim(mask_cols, key_first, key_span, 0)
        valid_keys = (mask_rows == 1) | (key_glob % 4 == 0)[:, None] & mark_cols[None, :]
        allowed = in_lat[:, None, :, None] & in_lon[None, :, None, :] & valid_keys[None, None, :, :]
        allowed = allowed.reshape(block_rows, block_keys)
        shifts = key_first - query_rows + (WIN - 1) + low_pad
        bias_parts = [
            lax.dynamic_slice_in_dim(table_pad, shifts[row_pos], key_span, 2)
            for row_pos in range(row_block)
        ]
        bias_rows = jnp.stack(bias_parts, axis=1).reshape(head_count, block_rows, block_keys)
        query_block = lax.dynamic_slice_in_dim(query_heads, local_first, row_block, 0).reshape(
            block_rows, head_count, HEAD_DIM
        )
        grad_block = lax.dynamic_slice_in_dim(grad_heads, local_first, row_block, 0).reshape(
            block_rows, head_count, HEAD_DIM
        )
        pair_block = lax.dynamic_slice_in_dim(extended, key_local, key_span, 1).reshape(
            2, block_keys, head_count, HEAD_DIM
        )
        key_block = pair_block[0]
        value_block = pair_block[1]
        scores = (
            score_scale
            * jnp.einsum("qhd,khd->hqk", query_block, key_block, preferred_element_type=jnp.float32)
            + bias_rows
        )
        scores = jnp.where(allowed[None], scores, -1e30)
        row_max = jnp.max(scores, axis=2, keepdims=True)
        weights_exp = jnp.exp(scores - row_max)
        prob_rows = weights_exp / jnp.sum(weights_exp, axis=2, keepdims=True)
        grad_prob = jnp.einsum(
            "qhd,khd->hqk", grad_block, value_block, preferred_element_type=jnp.float32
        )
        row_delta = jnp.sum(prob_rows * grad_prob, axis=2, keepdims=True)
        dscore = prob_rows * (grad_prob - row_delta)
        score_grid = dscore.reshape(head_count, row_block, lon_cols, key_span, ext_cols)
        score_grid = score_grid.transpose(0, 1, 3, 2, 4).reshape(
            head_count, row_block, key_span, lon_cols * ext_cols
        )
        for row_pos in range(row_block):
            prior_sum = lax.dynamic_slice_in_dim(table_acc, shifts[row_pos], key_span, 1)
            table_acc = lax.dynamic_update_slice_in_dim(
                table_acc, prior_sum + score_grid[:, row_pos], shifts[row_pos], 1
            )
        dscore_low = dscore.astype(jnp.bfloat16)
        prob_low = prob_rows.astype(jnp.bfloat16)
        grad_query = (
            score_scale
            * jnp.einsum("hqk,khd->qhd", dscore_low, key_block, preferred_element_type=jnp.float32)
        ).astype(jnp.bfloat16)
        key_part = score_scale * jnp.einsum(
            "hqk,qhd->khd", dscore_low, query_block, preferred_element_type=jnp.float32
        )
        value_part = jnp.einsum(
            "hqk,qhd->khd", prob_low, grad_block, preferred_element_type=jnp.float32
        )
        new_part = jnp.stack([key_part, value_part]).reshape(2, key_span, ext_cols, chan_width)
        prior_pair = lax.dynamic_slice_in_dim(grad_pair, key_local, key_span, 1)
        grad_pair = lax.dynamic_update_slice_in_dim(grad_pair, prior_pair + new_part, key_local, 1)
        return ((grad_pair, table_acc), grad_query)

    zero_pair = jnp.zeros((2, ext_rows, ext_cols, chan_width), jnp.float32)
    zero_table = jnp.zeros(
        (head_count, offset_rows + 2 * low_pad, lon_cols * ext_cols), jnp.float32
    )
    (grad_pair, table_acc), query_blocks = lax.scan(
        block_step, (zero_pair, zero_table), jnp.arange(block_count, dtype=jnp.int32)
    )
    grad_queries = query_blocks.reshape(lat_rows, lon_cols, chan_width)
    table_core = table_acc[:, low_pad : low_pad + offset_rows].reshape(
        head_count, offset_rows, lon_cols, ext_cols
    )
    col_take = (
        jnp.arange(lon_cols, dtype=jnp.int32)[:, None] + jnp.arange(WIN, dtype=jnp.int32)[None, :]
    )
    col_take = jnp.broadcast_to(
        col_take[None, None, :, :], (head_count, offset_rows, lon_cols, WIN)
    )
    table_local = jnp.sum(jnp.take_along_axis(table_core, col_take, axis=3), axis=2)
    grad_table = lax.psum(table_local, ("lat", "lon"))
    folded = fold_lat(fold_lon(grad_pair, lon_cols), lat_rows)
    grad_keys = folded[0].astype(jnp.bfloat16)
    grad_values = folded[1].astype(jnp.bfloat16)
    saved_out = attn_out.reshape(tokens, chan_width)
    slab_part = grad_cols
    grad_wout = lax.psum_scatter(
        jnp.dot(slab_part, saved_out, preferred_element_type=jnp.float32),
        ("lat", "lon"),
        scatter_dimension=0,
        tiled=True,
    )
    return (grad_queries, grad_keys, grad_values, grad_wout, grad_table)


def solution(mesh):
    return jax.shard_map(
        local,
        mesh=mesh,
        in_specs=(
            P("lat", "lon", "chan"),
            P("lat", "lon", "chan"),
            P("lat", "lon", "chan"),
            P("lat", "lon", "chan"),
            P("lat", "lon", "chan"),
            P(("lat", "lon"), "chan"),
            P("chan", None, None),
            P(),
        ),
        out_specs=(
            P("lat", "lon", "chan"),
            P("lat", "lon", "chan"),
            P("lat", "lon", "chan"),
            P(("lat", "lon"), "chan"),
            P("chan", None, None),
        ),
        check_vma=False,
    )
```

profile of v0, /device:TPU:240, one launch (start us, length us, event | category | flops | bytes accessed | tf_op | source)
XLA Modules:
  0.0 933.4 jit_solution(14924076082434811027)
XLA Ops:
  7.2 1.8 copy.63
  9.8 26.9 %all-gather.3.cloned.1.call-done = bf16[16,8,5120]{2,0,1:T(8,128)(2,1)} async-done(((bf16[16,8,1280]{2,0,1:T(8,128)(2,1)}), bf16[16,8,5120]{2,0,1:T(8,128)(2,1)}) %all-gather.3.cloned.1.call-update) | async-done | bytes 1310736 | tf_op jit(solution)/shard_map/all_gather | solution.py:79
  36.7 7.9 convolution_bitcast_fusion.1
  45.8 1.7 collective-permute-start.1
  51.5 4.6 collective-permute-start.3
  56.1 1.4 gather_fusion.1
  59.1 11.4 %collective-permute-done.3 = bf16[2,28,6,640]{3,0,2,1:T(2,128)(2,1)S(1)} collective-permute-done((bf16[2,28,6,640]{3,0,2,1:T(2,128)(2,1)S(1)}, bf16[2,28,6,640]{3,0,2,1:T(2,128)(2,1)S(1)}, u32[]{:S(2)}, u32[]{:S(2)}) %collective-permute-start.3) | collective-permute-done | bytes 430112 | tf_op jit(solution)/shard_map/ppermute | solution.py:18
  70.6 10.3 %collective-permute-done.2 = bf16[2,28,6,640]{3,0,2,1:T(2,128)(2,1)S(1)} collective-permute-done((bf16[2,28,6,640]{3,0,2,1:T(2,128)(2,1)S(1)}, bf16[2,28,6,640]{3,0,2,1:T(2,128)(2,1)S(1)}, u32[]{:S(2)}, u32[]{:S(2)}) %collective-permute-start.2) | collective-permute-done | bytes 430112 | tf_op jit(solution)/shard_map/ppermute | solution.py:17
  80.9 2.1 pad_maximum_fusion.1
  83.0 156.4 %all-gather.5.cloned.1.call-done = bf16[5120,640]{1,0:T(8,128)(2,1)} async-done(((bf16[80,640]{1,0:T(8,128)(2,1)}), bf16[5120,640]{1,0:T(8,128)(2,1)}) %all-gather.5.cloned.1.call-update) | async-done | bytes 6553616 | tf_op jit(solution)/shard_map/all_gather | solution.py:84
  239.4 4.6 fusion.42
  244.0 1.9 broadcast_in_dim.94
  245.9 117.0 %while.18 = (s32[]{:T(128)}, f32[2,28,20,640]{3,2,1,0:T(8,128)}, f32[5,31,160]{2,1,0:T(8,128)S(1)}, bf16[4,32,5,128]{3,1,2,0:T(8,128)(2,1)}, s32[4]{0:T(128)S(1)...) while((s32[]{:T(128)}, f32[2,28,20,640]{3,2,1,0:T(8,128)}, ...), condition=%wide.region_4.5_spmd.clone, body=%wide.region_0.0_spmd.clone.sunk | while | flops 67648624 | bytes 32509632 | solution.py:184
  257.6 1.3 constant_dynamic-slice_fusion.7
  259.8 1.9 dynamic-slice_bitcast_fusion.5
  272.1 3.0 fusion.106
  286.8 1.3 constant_dynamic-slice_fusion.7
  289.0 1.9 dynamic-slice_bitcast_fusion.5
  301.4 3.0 fusion.106
  316.0 1.3 constant_dynamic-slice_fusion.7
  318.3 1.9 dynamic-slice_bitcast_fusion.5
  330.6 3.1 fusion.106
  345.3 1.3 constant_dynamic-slice_fusion.7
  347.5 1.9 dynamic-slice_bitcast_fusion.5
  359.8 3.1 fusion.106
  363.0 2.2 convert.16
  367.6 2.0 collective-permute-start.4
  371.3 155.3 %gather_fusion.2 = f32[13000]{0:T(1024)S(1)} fusion(f32[5,25,8,20]{3,2,1,0:T(8,128)S(1)} %reshape.333, s32[13000]{0:T(1024)S(1)} %reshape.350), kind=kCustom, calls=%fused_computation.2 | custom fusion | bytes 312000 | tf_op jit(solution)/shard_map/jit(take_along_axis)/gather | solution.py:197
  529.9 2.3 fusion.59
  532.3 2.1 collective-permute-start.6
  534.3 4.4 collective-permute-start.7
  539.0 386.1 %psum.7 = f32[5,25,13]{2,1,0:T(8,128)S(1)} all-reduce(f32[5,25,13]{2,1,0:T(8,128)S(1)} %select_reduce_fusion), channel_id=1, replica_groups=mesh['lat'=8,'lon'=8,'chan'=4] {'lat','lon'}, use_global_device_ids=true, to_apply=%region_7.8 | all-reduce | flops 1625 | bytes 13000 | tf_op jit(solution)/shard_map/psum | solution.py:198
  (297 shorter events, 75.2 us)
Async XLA Ops:
  7.2 29.5 %copy-start = (bf16[16,8,640]{2,1,0:T(8,128)(2,1)S(1)}, bf16[16,8,640]{2,1,0:T(8,128)(2,1)}, u32[]{:S(2)}) copy-start(bf16[16,8,640]{2,1,0:T(8,128)(2,1)} %param.13) | copy-start | bytes 491524
  7.2 29.5 %all-gather.3.cloned.1.call-start = ((), (), s32[]{:S(2)}) async-start(), calls=%async_computation.1 | async-start | bytes 1638400 | tf_op jit(solution)/shard_map/all_gather | solution.py:79
  9.0 230.4 %all-gather.5.cloned.1.call-start = ((), (), s32[]{:S(2)}) async-start(), calls=%async_computation.2 | async-start | bytes 6656000 | tf_op jit(solution)/shard_map/all_gather | solution.py:84
  9.8 917.1 %reduce-scatter.2.cloned.1.call-start = ((), (), s32[]{:S(2)}) async-start(), calls=%async_computation.3 | async-start | bytes 13312000 | tf_op jit(solution)/shard_map/reduce_scatter | solution.py:204
  44.6 3.0 copy-start.8
  45.7 4.4 collective-permute-start
  45.8 4.8 collective-permute-start.1
  50.6 5.5 copy-start.1
  51.5 19.0 %collective-permute-start.3 = (bf16[2,28,6,640]{3,0,2,1:T(2,128)(2,1)S(1)}, bf16[2,28,6,640]{3,0,2,1:T(2,128)(2,1)S(1)}, u32[]{:S(2)}, u32[]{:S(2)}) collective-permute-start(bf16[2,28,6,640]{3,0,2,1:T(2,128)(2,1)S(1)} %copy.59), channel_id=1, source_target_pairs={{4,0},{8,4},{12,8},{16,12},{20,16},{24,20},{28,24},{0,28},{5,1},{9... | collective-permute-start | bytes 1290248 | tf_op jit(solution)/shard_map/ppermute | solution.py:18
  56.1 24.7 %collective-permute-start.2 = (bf16[2,28,6,640]{3,0,2,1:T(2,128)(2,1)S(1)}, bf16[2,28,6,640]{3,0,2,1:T(2,128)(2,1)S(1)}, u32[]{:S(2)}, u32[]{:S(2)}) collective-permute-start(bf16[2,28,6,640]{3,0,2,1:T(2,128)(2,1)S(1)} %copy.58), channel_id=1, source_target_pairs={{0,4},{4,8},{8,12},{12,16},{16,20},{20,24},{24,28},{28,0},{1,5},{5... | collective-permute-start | bytes 1290248 | tf_op jit(solution)/shard_map/ppermute | solution.py:17
  80.9 158.5 %copy-start.11 = (bf16[16,8,5120]{2,0,1:T(8,128)(2,1)S(1)}, bf16[16,8,5120]{2,0,1:T(8,128)(2,1)}, u32[]{:S(2)}) copy-start(bf16[16,8,5120]{2,0,1:T(8,128)(2,1)} %all-gather.3.cloned.1.call-done) | copy-start | bytes 3932164
  245.9 13.4 %copy-start.12 = (bf16[16,8,5,128]{3,1,2,0:T(8,128)(2,1)}, bf16[16,8,5,128]{3,1,2,0:T(8,128)(2,1)S(1)}, u32[]{:S(2)}) copy-start(bf16[16,8,5,128]{3,1,2,0:T(8,128)(2,1)S(1)} %get-tuple-element.541) | copy-start | bytes 491524 | tf_op jit(solution)/shard_map/while
  272.1 3.0 copy-start.13
  275.2 13.4 %copy-start.12 = (bf16[16,8,5,128]{3,1,2,0:T(8,128)(2,1)}, bf16[16,8,5,128]{3,1,2,0:T(8,128)(2,1)S(1)}, u32[]{:S(2)}) copy-start(bf16[16,8,5,128]{3,1,2,0:T(8,128)(2,1)S(1)} %get-tuple-element.541) | copy-start | bytes 491524 | tf_op jit(solution)/shard_map/while
  301.4 3.0 copy-start.13
  304.4 13.4 %copy-start.12 = (bf16[16,8,5,128]{3,1,2,0:T(8,128)(2,1)}, bf16[16,8,5,128]{3,1,2,0:T(8,128)(2,1)S(1)}, u32[]{:S(2)}) copy-start(bf16[16,8,5,128]{3,1,2,0:T(8,128)(2,1)S(1)} %get-tuple-element.541) | copy-start | bytes 491524 | tf_op jit(solution)/shard_map/while
  330.6 3.1 copy-start.13
  333.6 13.4 %copy-start.12 = (bf16[16,8,5,128]{3,1,2,0:T(8,128)(2,1)}, bf16[16,8,5,128]{3,1,2,0:T(8,128)(2,1)S(1)}, u32[]{:S(2)}) copy-start(bf16[16,8,5,128]{3,1,2,0:T(8,128)(2,1)S(1)} %get-tuple-element.541) | copy-start | bytes 491524 | tf_op jit(solution)/shard_map/while
  359.8 3.1 copy-start.13
  365.3 4.3 copy-start.4
  365.3 4.3 copy-start.6
  365.3 4.7 copy-start.14
  367.6 159.4 %collective-permute-start.5 = (bf16[2,28,6,640]{3,0,2,1:T(2,128)(2,1)}, bf16[2,28,6,640]{3,0,2,1:T(2,128)(2,1)}, u32[]{:S(2)}, u32[]{:S(2)}) collective-permute-start(bf16[2,28,6,640]{3,0,2,1:T(2,128)(2,1)} %copy.71), channel_id=1, source_target_pairs={{4,0},{8,4},{12,8},{16,12},{20,16},{24,20},{28,24},{0,28},{5,1},{9... | collective-permute-start | bytes 1290248 | tf_op jit(solution)/shard_map/ppermute | solution.py:18
  367.6 160.5 %collective-permute-start.4 = (bf16[2,28,6,640]{3,0,2,1:T(2,128)(2,1)}, bf16[2,28,6,640]{3,0,2,1:T(2,128)(2,1)}, u32[]{:S(2)}, u32[]{:S(2)}) collective-permute-start(bf16[2,28,6,640]{3,0,2,1:T(2,128)(2,1)} %copy.70), channel_id=1, source_target_pairs={{0,4},{4,8},{8,12},{12,16},{16,20},{20,24},{24,28},{28,0},{1,5},{5... | collective-permute-start | bytes 1290248 | tf_op jit(solution)/shard_map/ppermute | solution.py:17
  526.6 2.6 copy-start.5
  526.6 2.6 copy-start.7
  529.9 8.9 copy-start.16
  529.9 8.9 copy-start.18
  529.9 8.9 copy-start.20
  532.2 393.8 %copy-start.22 = (pred[16]{0:T(512)(128)(4,1)S(1)}, pred[16]{0:T(512)(128)(4,1)}, u32[]{:S(2)}) copy-start(pred[16]{0:T(512)(128)(4,1)} %constant.227.clone.1) | copy-start | bytes 52
  532.3 393.6 %collective-permute-start.6 = (bf16[2,6,8,640]{3,2,1,0:T(8,128)(2,1)S(1)}, bf16[2,6,8,640]{3,2,1,0:T(8,128)(2,1)S(1)}, u32[]{:S(2)}, u32[]{:S(2)}) collective-permute-start(bf16[2,6,8,640]{3,2,1,0:T(8,128)(2,1)S(1)} %get-tuple-element.361), channel_id=1, source_target_pairs={{0,32},{32,64},{64,96},{96,128},{128,160},{160,192},{192,224},{1,3... | collective-permute-start | bytes 368648 | tf_op jit(solution)/shard_map/ppermute | solution.py:17
  534.3 391.5 %collective-permute-start.7 = (bf16[2,6,8,640]{3,2,1,0:T(8,128)(2,1)S(1)}, bf16[2,6,8,640]{3,2,1,0:T(8,128)(2,1)S(1)}, u32[]{:S(2)}, u32[]{:S(2)}) collective-permute-start(bf16[2,6,8,640]{3,2,1,0:T(8,128)(2,1)S(1)} %get-tuple-element.362), channel_id=1, source_target_pairs={{32,0},{64,32},{96,64},{128,96},{160,128},{192,160},{224,192},{33,... | collective-permute-start | bytes 368648 | tf_op jit(solution)/shard_map/ppermute | solution.py:18
  (14 other events, 18.8 us)
Sparse Core Ops, SparseCore 0:
  9.8 26.8 all-gather.2
  38.5 200.8 all-gather.4
  242.6 461.3 reduce-scatter.1
where the time goes:
time: 935 us; the launch traced here: 933 us
  blocking collectives  386 us (41%)
  local copies, waits for them, and re-layouts  227 us (24%)
  waiting for transfers between devices  207 us (22%)
  loops' own time  33.7 us (4%)
  other arithmetic  28.7 us (3%)
  matrix products  21.7 us (2%)
  starting transfers between devices  15.1 us (2%)
  between operations  14.2 us (2%)
    psum x1, blocking collectives, local(): grad_table = lax.psum(table_local, ('lat', 'lon'))  386 us
    all_gather x1, waiting for transfers between devices, local(): lax.all_gather(w_out, ('lat', 'lon'), axis=0, tiled=True)  156 us
    gather x3, local copies, waits for them, and re-layouts, local(): jnp.take_along_axis(table_core, col_take, axis=3)  156 us
    another operation x1, loops' own time, local(): lax.scan(block_step, (zero_pair, zero_table), jnp.arange(block_count, dty...  33.7 us
    all_gather x1, waiting for transfers between devices, local(): lax.all_gather(grad_out, 'chan', axis=2, tiled=True).reshape(tokens, -1)  26.9 us
  transfers between devices with their start and end apart: 11, of which 6 were waited for; matrix products, arithmetic and copies ran while one was open for 29% of the time, Pallas kernels for 0%

commit v1 on v0

--- a/solution.py
+++ b/solution.py
@@ -5,6 +5,15 @@
 
 HEAD_DIM = 128
 WIN = 13
+
+
+def bars_balance(u_in):
+    return jnp.concatenate(
+        lax.all_to_all(
+            jnp.stack([u_in for _ in range(lax.axis_size(("lat", "lon")))]), ("lat", "lon"), 0, 0
+        ),
+        axis=0,
+    )
 
 
 def extended_2(value, sides, width, wrap):
@@ -80,10 +89,7 @@
     grad_cols = jnp.transpose(full_grad)
     slab_part = grad_cols
     grad_attn = lax.dot_general(
-        slab_part,
-        lax.all_gather(w_out, ("lat", "lon"), axis=0, tiled=True),
-        contract_lead,
-        preferred_element_type=jnp.float32,
+        slab_part, bars_balance(w_out), contract_lead, preferred_element_type=jnp.float32
     ).astype(jnp.bfloat16)
     kv_pair = jnp.stack([keys, values])
     extended = extended_2(kv_pair, (("lat", 1), ("lon", 2)), reach_cells, True)

time: 935 us -> 1020 us (1.091)
  starting transfers between devices: 15.1 us -> 69.5 us
  blocking collectives: 386 us -> 360 us
  local copies, waits for them, and re-layouts: 227 us -> 244 us
  waiting for transfers between devices: 207 us -> 223 us
  other arithmetic: 28.7 us -> 43.3 us
    ppermute x4, waiting for transfers between devices: 11.3 us -> 193 us  [extended_2(): before = lax.ppermute(last, axis, up)]
    all_gather x1 -> x0, waiting for transfers between devices: 156 us -> none  [local(): lax.all_gather(w_out, ('lat', 'lon'), axis=0, tiled=True)]
    ppermute x4, starting transfers between devices: 10.8 us -> 57.9 us  [extended_2(): after = lax.ppermute(leading, axis, down)]
    psum x1, blocking collectives: 386 us -> 360 us  [local(): grad_table = lax.psum(table_local, ('lat', 'lon'))]
    dynamic_update_slice x16, local copies, waits for them, and re-layouts: 3.93 us -> 25.7 us  [block_step(): lax.dynamic_update_slice_in_dim(table_acc, prior_sum + score_grid[:, row_...]
    add x16, other arithmetic: 0.35 us -> 14.7 us  [block_step(): prior_sum + score_grid[:, row_pos]]
    ppermute x4, waiting for transfers between devices: 11.9 us -> 0.01 us  [extended_2(): after = lax.ppermute(leading, axis, down)]
  transfers between devices with their start and end apart: 11 -> 11, of which waited for: 6 -> 3; matrix products, arithmetic and copies ran while one was open for 29% -> 30% of each run, Pallas kernels for 0% -> 0%
where the time goes in v1:
time: 1020 us; the launch traced here: 1010 us
  blocking collectives  360 us (35%)
  local copies, waits for them, and re-layouts  244 us (24%)
  waiting for transfers between devices  223 us (22%)
  starting transfers between devices  69.5 us (7%)
  other arithmetic  43.3 us (4%)
  loops' own time  33.3 us (3%)
  matrix products  25.8 us (3%)
  between operations  14.5 us (1%)
    psum x1, blocking collectives, local(): grad_table = lax.psum(table_local, ('lat', 'lon'))  360 us
    ppermute x4, waiting for transfers between devices, extended_2(): before = lax.ppermute(last, axis, up)  193 us
    gather x3, local copies, waits for them, and re-layouts, local(): jnp.take_along_axis(table_core, col_take, axis=3)  156 us
    ppermute x4, starting transfers between devices, extended_2(): after = lax.ppermute(leading, axis, down)  57.9 us
    another operation x1, loops' own time, local(): lax.scan(block_step, (zero_pair, zero_table), jnp.arange(block_count, dty...  33.3 us
    all_gather x1, waiting for transfers between devices, local(): lax.all_gather(grad_out, 'chan', axis=2, tiled=True).reshape(tokens, -1)  29.7 us
    dynamic_update_slice x16, local copies, waits for them, and re-layouts, block_step(): lax.dynamic_update_slice_in_dim(table_acc, prior_sum + score_grid[:, row_...  25.7 us
  transfers between devices with their start and end apart: 11, of which 3 were waited for; matrix products, arithmetic and copies ran while one was open for 30% of the time, Pallas kernels for 0%

profile of v1, /device:TPU:240, one launch (start us, length us, event | category | flops | bytes accessed | tf_op | source)
XLA Modules:
  0.0 1014.2 jit_solution(1577536986394125391)
XLA Ops:
  7.2 4.2 stack.47
  11.4 9.4 all-to-all-start
  21.7 29.7 %all-gather.2.cloned.1.call-done = bf16[16,8,5120]{2,0,1:T(8,128)(2,1)} async-done(((bf16[16,8,1280]{2,0,1:T(8,128)(2,1)}), bf16[16,8,5120]{2,0,1:T(8,128)(2,1)}) %all-gather.2.cloned.1.call-update) | async-done | bytes 1310736 | tf_op jit(solution)/shard_map/all_gather | solution.py:88
  51.4 7.9 convolution_bitcast_fusion.1
  60.5 1.7 collective-permute-start.1
  63.7 161.5 %collective-permute-done = bf16[2,6,8,640]{3,2,1,0:T(8,128)(2,1)S(1)} collective-permute-done((bf16[2,6,8,640]{3,2,1,0:T(8,128)(2,1)S(1)}, bf16[2,6,8,640]{3,2,1,0:T(8,128)(2,1)S(1)}, u32[]{:S(2)}, u32[]{:S(2)}) %collective-permute-start) | collective-permute-done | bytes 122912 | tf_op jit(solution)/shard_map/ppermute | solution.py:26
  226.3 44.5 %collective-permute-start.3 = (bf16[2,28,6,640]{3,0,2,1:T(2,128)(2,1)S(1)}, bf16[2,28,6,640]{3,0,2,1:T(2,128)(2,1)}, u32[]{:S(2)}, u32[]{:S(2)}) collective-permute-start(bf16[2,28,6,640]{3,0,2,1:T(2,128)(2,1)S(1)} %copy.59), channel_id=1, source_target_pairs={{4,0},{8,4},{12,8},{16,12},{20,16},{24,20},{28,24},{0,28},{5,1},{9... | collective-permute-start | bytes 1290248 | tf_op jit(solution)/shard_map/ppermute | solution.py:27
  272.9 31.8 %collective-permute-done.2 = bf16[2,28,6,640]{3,0,2,1:T(2,128)(2,1)S(1)} collective-permute-done((bf16[2,28,6,640]{3,0,2,1:T(2,128)(2,1)S(1)}, bf16[2,28,6,640]{3,0,2,1:T(2,128)(2,1)S(1)}, u32[]{:S(2)}, u32[]{:S(2)}) %collective-permute-start.2) | collective-permute-done | bytes 430112 | tf_op jit(solution)/shard_map/ppermute | solution.py:26
  305.9 2.0 pad_maximum_fusion.1
  308.0 5.1 fusion.42
  313.1 1.9 broadcast_in_dim.94
  315.7 147.0 %while.18 = (s32[]{:T(128)}, f32[2,28,20,640]{3,2,1,0:T(8,128)}, f32[5,31,160]{2,1,0:T(8,128)}, bf16[4,32,5,128]{3,1,2,0:T(8,128)(2,1)}, s32[4]{0:T(128)S(1)}, /...) while((s32[]{:T(128)}, f32[2,28,20,640]{3,2,1,0:T(8,128)}, ...), condition=%wide.region_4.5_spmd.clone, body=%wide.region_0.0_spmd.clone.sunk | while | flops 67648624 | bytes 28716212 | solution.py:190
  339.9 1.6 dynamic_update_slice.61
  342.5 1.6 dynamic_update_slice.62
  346.6 1.7 copy.122
  348.5 3.1 fusion.106
  376.7 1.6 dynamic_update_slice.61
  379.2 1.6 dynamic_update_slice.62
  383.4 1.7 copy.122
  385.3 3.1 fusion.106
  413.4 1.6 dynamic_update_slice.61
  420.1 1.7 copy.122
  422.0 3.1 fusion.106
  456.8 1.7 copy.122
  458.7 3.1 fusion.106
  462.7 2.2 convert.16
  467.3 8.0 collective-permute-start.5
  477.5 155.3 %gather_fusion.2 = f32[13000]{0:T(1024)S(1)} fusion(f32[5,25,8,20]{3,2,1,0:T(8,128)S(1)} %reshape.339, s32[13000]{0:T(1024)S(1)} %reshape.356), kind=kCustom, calls=%fused_computation.2 | custom fusion | bytes 312000 | tf_op jit(solution)/shard_map/jit(take_along_axis)/gather | solution.py:203
  636.1 2.4 fusion.59
  638.5 1.9 collective-permute-start.6
  640.4 3.6 collective-permute-start.7
  644.3 360.3 %psum.7 = f32[5,25,13]{2,1,0:T(8,128)S(1)} all-reduce(f32[5,25,13]{2,1,0:T(8,128)S(1)} %select_reduce_fusion), channel_id=1, replica_groups=mesh['lat'=8,'lon'=8,'chan'=4] {'lat','lon'}, use_global_device_ids=true, to_apply=%region_7.8 | all-reduce | flops 1625 | bytes 13000 | tf_op jit(solution)/shard_map/psum | solution.py:204
  (301 shorter events, 105.6 us)
Async XLA Ops:
  7.2 44.2 %copy-start = (bf16[16,8,640]{2,1,0:T(8,128)(2,1)S(1)}, bf16[16,8,640]{2,1,0:T(8,128)(2,1)}, u32[]{:S(2)}) copy-start(bf16[16,8,640]{2,1,0:T(8,128)(2,1)} %param.13) | copy-start | bytes 491524
  11.4 9.5 copy-start.15
  11.4 296.6 %all-to-all-start = ((bf16[64,80,640]{2,1,0:T(8,128)(2,1)}), bf16[64,80,640]{2,1,0:T(8,128)(2,1)}, u32[]{:S(2)}, u32[]{:S(2)}) async-start(bf16[64,80,640]{2,1,0:T(8,128)(2,1)} %stack.47), calls=%async_computation | async-start | bytes 13107200 | tf_op jit(solution)/shard_map/all_to_all | solution.py:12
  20.8 30.6 %all-gather.2.cloned.1.call-start = ((), (), s32[]{:S(2)}) async-start(), calls=%async_computation.2 | async-start | bytes 1638400 | tf_op jit(solution)/shard_map/all_gather | solution.py:88
  21.7 985.7 %reduce-scatter.2.cloned.1.call-start = ((), (), s32[]{:S(2)}) async-start(), calls=%async_computation.3 | async-start | bytes 13312000 | tf_op jit(solution)/shard_map/reduce_scatter | solution.py:210
  60.4 164.8 %collective-permute-start = (bf16[2,6,8,640]{3,2,1,0:T(8,128)(2,1)S(1)}, bf16[2,6,8,640]{3,2,1,0:T(8,128)(2,1)S(1)}, u32[]{:S(2)}, u32[]{:S(2)}) collective-permute-start(bf16[2,6,8,640]{3,2,1,0:T(8,128)(2,1)S(1)} %get-tuple-element.367), channel_id=1, source_target_pairs={{0,32},{32,64},{64,96},{96,128},{128,160},{160,192},{192,224},{224... | collective-permute-start | bytes 368648 | tf_op jit(solution)/shard_map/ppermute | solution.py:26
  60.5 164.8 %collective-permute-start.1 = (bf16[2,6,8,640]{3,2,1,0:T(8,128)(2,1)S(1)}, bf16[2,6,8,640]{3,2,1,0:T(8,128)(2,1)S(1)}, u32[]{:S(2)}, u32[]{:S(2)}) collective-permute-start(bf16[2,6,8,640]{3,2,1,0:T(8,128)(2,1)S(1)} %get-tuple-element.368), channel_id=1, source_target_pairs={{32,0},{64,32},{96,64},{128,96},{160,128},{192,160},{224,192},{0,2... | collective-permute-start | bytes 368648 | tf_op jit(solution)/shard_map/ppermute | solution.py:27
  225.3 45.5 %copy-start.2 = (f32[5,25,13]{1,2,0:T(8,128)S(1)}, f32[5,25,13]{1,2,0:T(8,128)}, u32[]{:S(2)}) copy-start(f32[5,25,13]{1,2,0:T(8,128)} %param.16) | copy-start | bytes 19504
  225.9 78.9 %collective-permute-start.2 = (bf16[2,28,6,640]{3,0,2,1:T(2,128)(2,1)S(1)}, bf16[2,28,6,640]{3,0,2,1:T(2,128)(2,1)S(1)}, u32[]{:S(2)}, u32[]{:S(2)}) collective-permute-start(bf16[2,28,6,640]{3,0,2,1:T(2,128)(2,1)S(1)} %copy.58), channel_id=1, source_target_pairs={{0,4},{4,8},{8,12},{12,16},{16,20},{20,24},{24,28},{28,0},{1,5},{5... | collective-permute-start | bytes 1290248 | tf_op jit(solution)/shard_map/ppermute | solution.py:26
  226.3 78.5 %collective-permute-start.3 = (bf16[2,28,6,640]{3,0,2,1:T(2,128)(2,1)S(1)}, bf16[2,28,6,640]{3,0,2,1:T(2,128)(2,1)}, u32[]{:S(2)}, u32[]{:S(2)}) collective-permute-start(bf16[2,28,6,640]{3,0,2,1:T(2,128)(2,1)S(1)} %copy.59), channel_id=1, source_target_pairs={{4,0},{8,4},{12,8},{16,12},{20,16},{24,20},{28,24},{0,28},{5,1},{9... | collective-permute-start | bytes 1290248 | tf_op jit(solution)/shard_map/ppermute | solution.py:27
  315.7 9.7 copy-start.5
  348.5 3.1 copy-start.4
  348.5 3.9 copy-start.6
  352.5 9.7 copy-start.5
  385.3 3.9 copy-start.6
  389.2 9.7 copy-start.5
  422.0 3.1 copy-start.4
  422.0 4.0 copy-start.6
  425.9 9.7 copy-start.5
  458.7 3.2 copy-start.4
  458.7 4.0 copy-start.6
  465.0 10.4 %copy-start.7 = (bf16[2,28,6,640]{3,2,1,0:T(8,128)(2,1)}, bf16[2,28,6,640]{3,2,1,0:T(8,128)(2,1)S(1)}, u32[]{:S(2)}) copy-start(bf16[2,28,6,640]{3,2,1,0:T(8,128)(2,1)S(1)} %get-tuple-element.359) | copy-start | bytes 1290244
  465.1 10.4 %copy-start.9 = (bf16[2,28,6,640]{3,2,1,0:T(8,128)(2,1)}, bf16[2,28,6,640]{3,2,1,0:T(8,128)(2,1)S(1)}, u32[]{:S(2)}) copy-start(bf16[2,28,6,640]{3,2,1,0:T(8,128)(2,1)S(1)} %get-tuple-element.360) | copy-start | bytes 1290244
  466.2 167.0 %collective-permute-start.4 = (bf16[2,28,6,640]{3,0,2,1:T(2,128)(2,1)}, bf16[2,28,6,640]{3,0,2,1:T(2,128)(2,1)}, u32[]{:S(2)}, u32[]{:S(2)}) collective-permute-start(bf16[2,28,6,640]{3,0,2,1:T(2,128)(2,1)} %copy.70), channel_id=1, source_target_pairs={{0,4},{4,8},{8,12},{12,16},{16,20},{20,24},{24,28},{28,0},{1,5},{5... | collective-permute-start | bytes 1290248 | tf_op jit(solution)/shard_map/ppermute | solution.py:26
  467.3 167.0 %collective-permute-start.5 = (bf16[2,28,6,640]{3,0,2,1:T(2,128)(2,1)}, bf16[2,28,6,640]{3,0,2,1:T(2,128)(2,1)}, u32[]{:S(2)}, u32[]{:S(2)}) collective-permute-start(bf16[2,28,6,640]{3,0,2,1:T(2,128)(2,1)} %copy.71), channel_id=1, source_target_pairs={{4,0},{8,4},{12,8},{16,12},{20,16},{24,20},{28,24},{0,28},{5,1},{9... | collective-permute-start | bytes 1290248 | tf_op jit(solution)/shard_map/ppermute | solution.py:27
  636.1 8.0 copy-start.18
  636.1 8.0 copy-start.20
  636.1 8.0 copy-start.22
  636.1 369.3 %copy-start.16 = (bf16[4,32,5,128]{3,1,2,0:T(8,128)(2,1)S(1)}, bf16[4,32,5,128]{3,1,2,0:T(8,128)(2,1)}, u32[]{:S(2)}) copy-start(bf16[4,32,5,128]{3,1,2,0:T(8,128)(2,1)} %get-tuple-element.218) | copy-start | bytes 491524
  638.5 367.8 %collective-permute-start.6 = (bf16[2,6,8,640]{3,2,1,0:T(8,128)(2,1)S(1)}, bf16[2,6,8,640]{3,2,1,0:T(8,128)(2,1)S(1)}, u32[]{:S(2)}, u32[]{:S(2)}) collective-permute-start(bf16[2,6,8,640]{3,2,1,0:T(8,128)(2,1)S(1)} %get-tuple-element.361), channel_id=1, source_target_pairs={{0,32},{32,64},{64,96},{96,128},{128,160},{160,192},{192,224},{1,3... | collective-permute-start | bytes 368648 | tf_op jit(solution)/shard_map/ppermute | solution.py:26
  640.4 365.9 %collective-permute-start.7 = (bf16[2,6,8,640]{3,2,1,0:T(8,128)(2,1)S(1)}, bf16[2,6,8,640]{3,2,1,0:T(8,128)(2,1)S(1)}, u32[]{:S(2)}, u32[]{:S(2)}) collective-permute-start(bf16[2,6,8,640]{3,2,1,0:T(8,128)(2,1)S(1)} %get-tuple-element.362), channel_id=1, source_target_pairs={{32,0},{64,32},{96,64},{128,96},{160,128},{192,160},{224,192},{33,... | collective-permute-start | bytes 368648 | tf_op jit(solution)/shard_map/ppermute | solution.py:27
  644.3 362.2 %copy-start.24 = (pred[16]{0:T(512)(128)(4,1)S(1)}, pred[16]{0:T(512)(128)(4,1)}, u32[]{:S(2)}) copy-start(pred[16]{0:T(512)(128)(4,1)} %constant.227.clone.1) | copy-start | bytes 52
  (16 other events, 30.2 us)
Sparse Core Ops, SparseCore 0:
  23.4 27.9 all-gather.1
  59.5 554.8 reduce-scatter.1
